TPU v7x, 32 devices: a whole 2x2x4 slice. The times are simulated.
32 devices in a mesh: rot: 8 (over y, x, core), az: 4 (over z).
Axes of the slice: x: 2, y: 2, z: 4, core: 2. Of those that a mesh axis runs over, the one named last changes fastest.
Arguments:
- inputs: bfloat16 [16, 4, 128, 128], P('rot', None, 'az'), may hold values from -6 to 6
- pre_one: bfloat16 [16, 4, 128, 128], P('rot', None, 'az'), may hold values from -8 to 8
- pre_two: bfloat16 [16, 4, 128, 128], P('rot', None, 'az'), may hold values from -8 to 8
- cotangent: bfloat16 [16, 4, 128, 128], P('rot', None, 'az'), may hold values from -6 to 6
- filt_one: bfloat16 [16, 3, 3, 128, 128], P('rot'), may hold values from -0.046875 to 0.046875
- filt_two: bfloat16 [16, 3, 3, 128, 128], P('rot'), may hold values from -0.046875 to 0.046875
Outputs:
- input_grad: bfloat16 [16, 4, 128, 128], P('rot', None, 'az')
- filt_grad_one: float32 [16, 3, 3, 128, 128], P('rot')
- filt_grad_two: float32 [16, 3, 3, 128, 128], P('rot')
All inputs are finite; a program needn't handle non-finite values.
Results may differ from a plain program's by a relative error of at most 0.018.
Values may be sent and summed in bfloat16 or wider, within the bound.
A program may use at most 64 MiB of HBM per device.

v0:
```python
import functools

import jax
import jax.numpy as jnp
from jax import lax
from jax.experimental import pallas as pl
from jax.experimental.pallas import tpu as pltpu
from jax.sharding import PartitionSpec as P

F32 = jnp.float32
BF16 = jnp.bfloat16


def slope(v):
    s = jax.nn.sigmoid(v)
    return s * (1.0 + v * (1.0 - s))


def kernel(
    n, m, p, H, X, C,
    inputs, pre_one, pre_two, cot, filt_one, filt_two,
    out_in, out_f1, out_f2,
    st_g, st_e, st_a, grads, edges, feats, weights, gx, lhs, outs,
    part_s, part_x, part_m, part_r, zs, zr, zt,
    g_ss, g_rs, gf_ss, gf_rs, e_ss, e_rs, ef_ss, ef_rs, a_ss, a_rs, af_ss, af_rs,
    x_ss, x_rs, p_ss, p_rs, z_ss, z_rs, y_ss, y_rs,
):
    R = n * p
    HX = H * X
    nc = n // 2
    K = 9 * p
    me = lax.axis_index("rot")
    z = lax.axis_index("az")
    core = lax.rem(me, 2)
    chip = lax.div(me, 2)
    sib = me + 1 - 2 * core

    def to(t):
        return 2 * lax.rem(chip + t, nc) + core

    def frm(t):
        return 2 * lax.rem(chip + nc - t, nc) + core

    def col(d):
        return lax.rem(z + d, m)

    def copy(src, dst, ss, rs, rot, az):
        return pltpu.make_async_remote_copy(
            src_ref=src, dst_ref=dst, send_sem=ss, recv_sem=rs,
            device_id={"rot": rot, "az": az}, device_id_type=pl.DeviceIdType.MESH,
        )

    barrier = pltpu.get_barrier_semaphore()
    near_cols = sorted({1 % m, (m - 1) % m})
    partners = [(sib, z)] + [(to(t), z) for t in range(1, nc)]
    partners += [(to(t), col(d)) for d in near_cols for t in range(nc)]
    for rot, az in partners:
        pl.semaphore_signal(
            barrier, inc=1, device_id={"rot": rot, "az": az},
            device_id_type=pl.DeviceIdType.MESH,
        )

    pending = []

    def start(c):
        c.start()
        pending.append(c)
        return c

    def stage_grad(ph, value):
        st_g[ph] = value.astype(BF16)
        grads[ph, me] = value.astype(BF16)
        st_e[ph, 0] = value[:, :, 0, :].reshape(p * H, C).astype(BF16)
        st_e[ph, 1] = value[:, :, X - 1, :].reshape(p * H, C).astype(BF16)

    def send_grad(ph):
        direct = [None] + [
            start(copy(st_g.at[ph], grads.at[ph, me], g_ss.at[ph, t], g_rs.at[ph, t], to(t), z))
            for t in range(1, nc)
        ]
        own = start(copy(st_g.at[ph], grads.at[ph, me], gf_ss.at[ph, 0], gf_rs.at[ph, 0], sib, z))
        rims = []
        for t in range(nc):
            for side, d in ((1, 1), (0, m - 1)):
                rims.append(
                    start(
                        copy(
                            st_e.at[ph, side], edges.at[ph, me, 1 - side],
                            e_ss.at[ph, side, t], e_rs.at[ph, side, t], to(t), col(d),
                        )
                    )
                )
        return direct, own, rims

    def relay_grad(ph, sent):
        direct, own, rims = sent
        passed = [own]
        for t in range(nc):
            rims[2 * t].wait_recv()
            rims[2 * t + 1].wait_recv()
            d = frm(t)
            passed.append(
                start(copy(edges.at[ph, d], edges.at[ph, d], ef_ss.at[ph, t], ef_rs.at[ph, t], sib, z))
            )
        for t in range(1, nc):
            direct[t].wait_recv()
            d = frm(t)
            passed.append(
                start(copy(grads.at[ph, d], grads.at[ph, d], gf_ss.at[ph, t], gf_rs.at[ph, t], sib, z))
            )
        return passed

    def stage_feat(ph, value):
        for o in range(p):
            turned = value[o].T.astype(BF16)
            st_a[ph, o] = turned
            feats[ph, me, o] = turned

    def send_feat(ph):
        direct = [None] + [
            start(copy(st_a.at[ph], feats.at[ph, me], a_ss.at[ph, t], a_rs.at[ph, t], to(t), z))
            for t in range(1, nc)
        ]
        own = start(copy(st_a.at[ph], feats.at[ph, me], af_ss.at[ph, 0], af_rs.at[ph, 0], sib, z))
        return direct, own

    def relay_feat(ph, sent):
        direct, own = sent
        passed = [own]
        for t in range(1, nc):
            direct[t].wait_recv()
            d = frm(t)
            passed.append(
                start(copy(feats.at[ph, d], feats.at[ph, d], af_ss.at[ph, t], af_rs.at[ph, t], sib, z))
            )
        return passed

    def arrive(copies):
        for c in copies:
            c.wait_recv()

    def build_gx(ph):
        x_of = lax.broadcasted_iota(jnp.int32, (p * H, X, C), 1).reshape(p * HX, C)

        def body(d, carry):
            g = grads[ph, d].astype(F32).reshape(p * HX, C)
            low = edges[ph, d, 0].astype(F32)
            high = edges[ph, d, 1].astype(F32)
            low = jnp.broadcast_to(low[:, None, :], (p * H, X, C)).reshape(p * HX, C)
            high = jnp.broadcast_to(high[:, None, :], (p * H, X, C)).reshape(p * HX, C)
            before = jnp.where(x_of == 0, low, pltpu.roll(g, 1, 0))
            after = jnp.where(x_of == X - 1, high, pltpu.roll(g, p * HX - 1, 0))
            for j, v in enumerate((after, g, before)):
                gx[pl.ds(d * p, p), 1 : H + 1, :, j * C : (j + 1) * C] = v.astype(BF16).reshape(p, H, X, C)
            return carry

        lax.fori_loop(0, n, body, 0)

    def build_weights(filt):
        for s in range(p):
            for i in range(3):
                for j in range(3):
                    weights[s * C : (s + 1) * C, (i * 3 + j) * C : (i * 3 + j + 1) * C] = filt[s, i, j]

    def build_lhs(ph):
        lane = lax.broadcasted_iota(jnp.int32, (C, HX), 1)
        for q in range(n):
            owner = lax.rem(me + q, n)
            for o in range(p):
                block = q * p + o
                a = feats[ph, owner, o]
                wide = a.astype(F32)
                down = jnp.where(lane < X, 0.0, pltpu.roll(wide, X, 1)).astype(BF16)
                up = jnp.where(lane >= HX - X, 0.0, pltpu.roll(wide, HX - X, 1)).astype(BF16)
                spots = [block] + ([R + block] if block < p - 1 else [])
                for spot in spots:
                    for i, v in enumerate((down, a, up)):
                        lhs[i * C : (i + 1) * C, spot * HX : (spot + 1) * HX] = v

    def term(q, o):
        total = None
        for s in range(p):
            one = outs[(q * p + o - s) % R, :, s * C : (s + 1) * C]
            total = one if total is None else total + one
        return total

    def data_terms(ph):
        w = weights[...]
        crossed = [None] * n

        def emit(q):
            for o in range(p):
                part_s[ph, q, o] = term(q, o).astype(BF16)
            t = lax.rem(q // 2 + core, nc)
            crossed[q] = start(
                copy(part_s.at[ph, q], part_x.at[ph, t], x_ss.at[ph, t], x_rs.at[ph, t], sib, z)
            )

        for q in range(n):
            rows = jnp.concatenate(
                [gx[q * p : (q + 1) * p, 2 - i : 2 - i + H].reshape(p * HX, 3 * C) for i in range(3)],
                axis=1,
            )
            got = lax.dot_general(rows, w, (((1,), (1,)), ((), ())), preferred_element_type=F32)
            outs[q * p : (q + 1) * p] = got.reshape(p, HX, p * C)
            if q % 2 == 1:
                emit(q)

    def merge_terms(ph):
        sent = []
        for t in list(range(1, nc)) + [0]:
            pltpu.make_async_remote_copy(
                src_ref=part_x.at[ph, t], dst_ref=part_x.at[ph, t],
                send_sem=x_ss.at[ph, t], recv_sem=x_rs.at[ph, t],
                device_id={"rot": sib, "az": z}, device_id_type=pl.DeviceIdType.MESH,
            ).wait_recv()
            for o in range(p):
                total = term(2 * t, o) + part_x[ph, t, o].astype(F32)
                if t == 0:
                    part_r[ph, 0, o] = total.astype(BF16)
                else:
                    part_m[ph, t, o] = total.astype(BF16)
            if t > 0:
                sent.append(
                    start(
                        copy(part_m.at[ph, t], part_r.at[ph, t], p_ss.at[ph, t], p_rs.at[ph, t], to(t), z)
                    )
                )
        return sent

    def part_sum(ph, copies):
        arrive(copies)
        total = part_r[ph, 0].astype(F32)
        for t in range(1, nc):
            total = total + part_r[ph, t].astype(F32)
        return total

    fg = (out_f2, out_f1)
    lower = z < m // 2
    near_pos = jnp.where(lower, z, m - 1 - z)
    right, left = jnp.minimum(z + 1, m - 1), jnp.maximum(z - 1, 0)
    inner = jnp.where(lower, right, left)
    outer = jnp.where(lower, left, right)
    at_end = near_pos == 0
    at_mid = near_pos == m // 2 - 1
    slot = jnp.where(at_mid, 1, 0)

    def inward(src, ph, k):
        return copy(src, zr.at[ph, slot, k], z_ss.at[ph, k], z_rs.at[ph, slot, k], me, inner)

    def crossed_in(ph, w, k):
        return copy(zr.at[ph, w, k], zr.at[ph, w, k], z_ss.at[ph, k], z_rs.at[ph, w, k], me, inner)

    def outward(ph, k):
        return copy(fg[ph].at[k], fg[ph].at[k], y_ss.at[ph, k], y_rs.at[ph, k], me, outer)

    def filt_terms(ph):
        right_side = gx[:, 1 : H + 1].reshape(R * HX, 3 * C)
        for s in range(p):
            got = jnp.dot(
                lhs[:, s * HX : (s + R) * HX], right_side, preferred_element_type=F32
            )
            for i in range(3):
                for j in range(3):
                    zs[ph, (s * 3 + i) * 3 + j] = got[i * C : (i + 1) * C, j * C : (j + 1) * C].astype(BF16)

            if ph == 1:
                begin(ph, s * 18 // p, (s + 1) * 18 // p)

    def begin(ph, a, b):
        @pl.when(at_end)
        def _():
            for k in range(K * a // 18, K * b // 18):
                inward(zs.at[ph, k], ph, k).start()

    def go_in(ph, a, b):
        @pl.when(jnp.logical_not(at_end))
        def _():
            for k in range(K * a // 18, K * b // 18):
                crossed_in(ph, 0, k).wait_recv()
                zt[ph, k] = (zs[ph, k].astype(F32) + zr[ph, 0, k].astype(F32)).astype(BF16)
                inward(zt.at[ph, k], ph, k).start()

    base = zs if m == 2 else zt

    def go_out(ph, a, b):
        for k in range(K * a // 18, K * b // 18):

            @pl.when(at_mid)
            def _():
                crossed_in(ph, 1, k).wait_recv()
                fg[ph][k] = (base[ph, k].astype(F32) + zr[ph, 1, k].astype(F32)).astype(BF16)

            @pl.when(jnp.logical_not(at_mid))
            def _():
                outward(ph, k).wait_recv()

            @pl.when(jnp.logical_not(at_end))
            def _():
                outward(ph, k).start()

    def drain(ph):
        for k in range(K):
            crossed_in(ph, 0, k).wait_send()

        @pl.when(jnp.logical_not(at_end))
        def _():
            for k in range(K):
                outward(ph, k).wait_send()

    grad_two = (cot[...].astype(F32) * slope(pre_two[...].astype(F32))).astype(BF16).astype(F32)
    stage_grad(0, grad_two)
    pl.semaphore_wait(barrier, len(partners))
    g_sent = send_grad(0)
    wide_one = pre_one[...].astype(F32)
    stage_feat(0, (wide_one * jax.nn.sigmoid(wide_one)).reshape(p, HX, C))
    a_sent = send_feat(0)
    stage_feat(1, inputs[...].astype(F32).reshape(p, HX, C))
    build_weights(filt_two)
    gx[:, 0] = jnp.zeros((R, X, 3 * C), BF16)
    gx[:, H + 1] = jnp.zeros((R, X, 3 * C), BF16)
    arrive(relay_grad(0, g_sent))
    build_gx(0)
    data_terms(0)
    a_passed = relay_feat(0, a_sent)
    p_sent = merge_terms(0)
    i_sent = send_feat(1)
    arrive(a_passed)
    build_lhs(0)
    filt_terms(0)
    begin(0, 0, 6)

    delta = part_sum(0, p_sent).reshape(p, H, X, C)
    grad_one = (delta * slope(pre_one[...].astype(F32))).astype(BF16).astype(F32)
    stage_grad(1, grad_one)
    g_sent = send_grad(1)
    begin(0, 6, 18)
    i_passed = relay_feat(1, i_sent)
    go_in(0, 0, 2)
    build_weights(filt_one)
    arrive(i_passed)
    build_lhs(1)
    go_in(0, 2, 6)
    g_passed = relay_grad(1, g_sent)
    go_in(0, 6, 9)
    go_out(0, 0, 3)
    arrive(g_passed)
    build_gx(1)
    go_in(0, 9, 12)
    go_out(0, 3, 7)
    filt_terms(1)
    go_in(0, 12, 16)
    go_out(0, 7, 12)
    data_terms(1)
    go_in(0, 16, 18)
    p_sent = merge_terms(1)
    go_out(0, 12, 18)
    go_in(1, 0, 4)
    out_in[...] = part_sum(1, p_sent).astype(BF16).reshape(p, H, X, C)
    for k in range(4, 18):
        go_in(1, k, k + 1)
        go_out(1, k - 4, k - 3)
    go_out(1, 14, 18)
    for c in pending:
        c.wait_send()
    drain(0)
    drain(1)


def solution(mesh):
    n, m = mesh.shape["rot"], mesh.shape["az"]

    def shards(inputs, pre_one, pre_two, cot, filt_one, filt_two):
        p, H, X, C = inputs.shape
        R, HX, K, nc = n * p, H * X, 9 * p, n // 2
        scale = float(R * H * X * m) ** -0.5
        dma = pltpu.SemaphoreType.DMA
        vmem = pl.BlockSpec(memory_space=pltpu.VMEM)
        sums = jax.ShapeDtypeStruct((K, C, C), BF16)
        got, sum_one, sum_two = pl.pallas_call(
            functools.partial(kernel, n, m, p, H, X, C),
            out_shape=(jax.ShapeDtypeStruct((p, H, X, C), BF16), sums, sums),
            in_specs=[vmem] * 6,
            out_specs=(vmem,) * 3,
            scratch_shapes=[
                pltpu.VMEM((2, p, H, X, C), BF16),
                pltpu.VMEM((2, 2, p * H, C), BF16),
                pltpu.VMEM((2, p, C, HX), BF16),
                pltpu.VMEM((2, n, p, H, X, C), BF16),
                pltpu.VMEM((2, n, 2, p * H, C), BF16),
                pltpu.VMEM((2, n, p, C, HX), BF16),
                pltpu.VMEM((p * C, 9 * C), BF16),
                pltpu.VMEM((R, H + 2, X, 3 * C), BF16),
                pltpu.VMEM((3 * C, (R + p - 1) * HX), BF16),
                pltpu.VMEM((R, HX, p * C), F32),
                pltpu.VMEM((2, n, p, HX, C), BF16),
                pltpu.VMEM((2, nc, p, HX, C), BF16),
                pltpu.VMEM((2, nc, p, HX, C), BF16),
                pltpu.VMEM((2, nc, p, HX, C), BF16),
                pltpu.VMEM((2, K, C, C), BF16),
                pltpu.VMEM((2, 2, K, C, C), BF16),
                pltpu.VMEM((2, K, C, C), BF16),
            ]
            + [dma((2, nc))] * 4
            + [dma((2, 2, nc))] * 2
            + [dma((2, nc))] * 2
            + [dma((2, nc))] * 8
            + [dma((2, K)), dma((2, 2, K)), dma((2, K)), dma((2, K))],
            compiler_params=pltpu.CompilerParams(
                collective_id=0, has_side_effects=True, vmem_limit_bytes=60 * 1024 * 1024
            ),
        )(inputs, pre_one, pre_two, cot, filt_one, filt_two)

        def widen(v):
            return (v.astype(F32) * scale).reshape(p, 3, 3, C, C)

        return got, widen(sum_one), widen(sum_two)

    cells = P("rot", None, "az", None)
    banks = P("rot", None, None, None, None)
    return jax.shard_map(
        shards, mesh=mesh,
        in_specs=(cells,) * 4 + (banks,) * 2,
        out_specs=(cells, banks, banks),
        check_vma=False,
    )
```

profile of v0, /device:TPU:0, one launch (start us, length us, event | category | flops | bytes accessed | tf_op | source)
XLA Modules:
  0.0 65.7 jit_solution(17255144214107877661)
XLA Ops:
  0.6 61.4 %shard_map.85 = (bf16[2,4,32,128]{3,2,1,0:T(8,128)(2,1)}, bf16[18,128,128]{2,1,0:T(8,128)(2,1)}, bf16[18,128,128]{2,1,0:T(8,128)(2,1)}) custom-call(bf16[2,4,32,128]{3,2,1,0:T(8,128)(2,1)} %inputs.1, bf16[2,4,32,128]{3,2,1,0:T(8,128)(2,1)} %pre_one.1, bf16[2,4,32,128]{3,2,1,0:T(8,128)(2,1)} %pre_two.1, bf16[2,4,32,128]{3,2,1,0:T(8,128)(2,1)} %cot.1, ...), custom_call_target="tpu_custom_call" | custom-call | tf_op jit(solution)/shard_map/pallas_call | solution.py:380
  62.1 0.0 copy-start
  62.1 3.0 %convert_multiply_fusion = (f32[18,128,128]{2,1,0:T(8,128)}, f32[18,128,128]{2,1,0:T(8,128)}) fusion(bf16[18,128,128]{2,1,0:T(8,128)(2,1)} %get-tuple-element.8, bf16[18,128,128]{2,1,0:T(8,128)(2,1)} %get-tuple-element.7), kind=kLoop, calls=%fused_computation | loop fusion | flops 1179648 | bytes 3538944 | tf_op jit(solution)/shard_map/mul | solution.py:415
  65.0 0.0 copy-done
  65.0 0.6 copy.10
Async XLA Ops:
  62.1 3.0 %copy-start = (bf16[2,4,32,128]{3,2,1,0:T(8,128)(2,1)S(1)}, bf16[2,4,32,128]{3,2,1,0:T(8,128)(2,1)}, u32[]{:S(2)}) copy-start(bf16[2,4,32,128]{3,2,1,0:T(8,128)(2,1)} %get-tuple-element.14) | copy-start | bytes 196612
where the time goes:
time: 65.8 us; the launch traced here: 65.7 us
  Pallas kernels  61.4 us (93%)
  other arithmetic  2.96 us (4%)
    pallas_call x1, Pallas kernels, shards(): pl.pallas_call(functools.partial(kernel, n, m, p, H, X, C), out_shape=(ja...  61.4 us
    mul x1, other arithmetic, widen(): return (v.astype(F32) * scale).reshape(p, 3, 3, C, C)  2.96 us

commit v1 on v0

v1 whole, which is shorter than its diff:
```python
import functools

import jax
import jax.numpy as jnp
from jax import lax
from jax.experimental import pallas as pl
from jax.experimental.pallas import tpu as pltpu
from jax.sharding import PartitionSpec as P

F32 = jnp.float32
BF16 = jnp.bfloat16


def slope(v):
    s = jax.nn.sigmoid(v)
    return s * (1.0 + v * (1.0 - s))


def kernel(
    n, m, p, H, X, C, scale,
    inputs, pre_one, pre_two, cot, filt_one, filt_two,
    out_in, out_f1, out_f2,
    st_g, st_e, st_a, grads, edges, feats, weights, gx, lhs, outs,
    part_s, part_x, part_m, part_r, zs, zr, zt, zf,
    col_in, st_t, whole_in, whole_g, acc, turn,
    g_ss, g_rs, gf_ss, gf_rs, e_ss, e_rs, ef_ss, ef_rs, a_ss, a_rs, af_ss, af_rs,
    x_ss, x_rs, p_ss, p_rs, z_ss, z_rs, y_ss, y_rs,
    w_sem, iz_ss, iz_rs, gz_ss, gz_rs, h_ss, h_rs, hf_ss, hf_rs,
):
    R = n * p
    HX = H * X
    nc = n // 2
    K = 9 * p
    AZ = m * X
    span = p * H * AZ
    me = lax.axis_index("rot")
    z = lax.axis_index("az")
    core = lax.rem(me, 2)
    chip = lax.div(me, 2)
    sib = me + 1 - 2 * core

    def to(t):
        return 2 * lax.rem(chip + t, nc) + core

    def frm(t):
        return 2 * lax.rem(chip + nc - t, nc) + core

    def col(d):
        return lax.rem(z + d, m)

    def col_at(zz):
        return pl.ds(pl.multiple_of(zz * X, X), X)

    def g_at(owner, target_chip):
        return pl.ds(p * lax.rem(owner - 2 * target_chip + n, n), p)

    def a_at(owner, target):
        slot = lax.rem(owner - 2 * lax.div(target, 2) - target + 2 * n, n)
        return pl.ds(pl.multiple_of(slot * span, span), span)

    def copy(src, dst, ss, rs, rot, az):
        return pltpu.make_async_remote_copy(
            src_ref=src, dst_ref=dst, send_sem=ss, recv_sem=rs,
            device_id={"rot": rot, "az": az}, device_id_type=pl.DeviceIdType.MESH,
        )

    loads = [
        [
            pltpu.make_async_copy(
                filt.at[s, i, j],
                weights.at[l, pl.ds(s * C, C), pl.ds((i * 3 + j) * C, C)],
                w_sem.at[l, (s * 3 + i) * 3 + j],
            )
            for s in range(p) for i in range(3) for j in range(3)
        ]
        for l, filt in enumerate((filt_two, filt_one))
    ]
    for load in loads[0] + loads[1]:
        load.start()

    barrier = pltpu.get_barrier_semaphore()
    near_cols = sorted({1 % m, (m - 1) % m})
    partners = [(sib, z)] + [(to(t), z) for t in range(1, nc)]
    partners += [(to(t), col(d)) for d in near_cols for t in range(nc)]
    partners += [(me, col(d)) for d in range(1, m) if d not in near_cols]
    for rot, az in partners:
        pl.semaphore_signal(
            barrier, inc=1, device_id={"rot": rot, "az": az},
            device_id_type=pl.DeviceIdType.MESH,
        )

    pending = []

    def start(c):
        c.start()
        pending.append(c)
        return c

    def stage_grad(ph, value):
        st_g[ph] = value.astype(BF16)
        if ph == 0:
            grads[me] = value.astype(BF16)
        else:
            whole_g[g_at(me, chip), :, col_at(z), :] = value.astype(BF16)
        st_e[ph, 0] = value[:, :, 0, :].reshape(p * H, C).astype(BF16)
        st_e[ph, 1] = value[:, :, X - 1, :].reshape(p * H, C).astype(BF16)

    def home(ph, owner, target_chip, zz):
        if ph == 0:
            return grads.at[owner]
        return whole_g.at[g_at(owner, target_chip), :, col_at(zz), :]

    def there(t):
        return lax.rem(chip + t, nc)

    def send_grad(ph):
        rims = []
        for t in range(nc):
            for side, d in ((1, 1), (0, m - 1)):
                rims.append(
                    start(
                        copy(
                            st_e.at[ph, side], edges.at[ph, me, 1 - side],
                            e_ss.at[ph, side, t], e_rs.at[ph, side, t], to(t), col(d),
                        )
                    )
                )
        direct = [None] + [
            start(copy(st_g.at[ph], home(ph, me, there(t), z), g_ss.at[ph, t], g_rs.at[ph, t], to(t), z))
            for t in range(1, nc)
        ]
        own = start(copy(st_g.at[ph], home(ph, me, chip, z), gf_ss.at[ph, 0], gf_rs.at[ph, 0], sib, z))
        return direct, own, rims

    def relay_grad(ph, sent):
        direct, own, rims = sent
        passed = [own]
        for t in range(nc):
            rims[2 * t].wait_recv()
            rims[2 * t + 1].wait_recv()
            d = frm(t)
            passed.append(
                start(copy(edges.at[ph, d], edges.at[ph, d], ef_ss.at[ph, t], ef_rs.at[ph, t], sib, z))
            )
        for t in range(1, nc):
            direct[t].wait_recv()
            d = frm(t)
            passed.append(
                start(copy(home(ph, d, chip, z), home(ph, d, chip, z), gf_ss.at[ph, t], gf_rs.at[ph, t], sib, z))
            )
        return passed

    def stage_feat(value):
        for o in range(p):
            turned = value[o].T.astype(BF16)
            st_a[o] = turned
            feats[me, o] = turned

    def send_feat():
        direct = [None] + [
            start(copy(st_a, feats.at[me], a_ss.at[0, t], a_rs.at[0, t], to(t), z))
            for t in range(1, nc)
        ]
        own = start(copy(st_a, feats.at[me], af_ss.at[0, 0], af_rs.at[0, 0], sib, z))
        return direct, own

    def relay_feat(sent):
        direct, own = sent
        passed = [own]
        for t in range(1, nc):
            direct[t].wait_recv()
            d = frm(t)
            passed.append(
                start(copy(feats.at[d], feats.at[d], af_ss.at[0, t], af_rs.at[0, t], sib, z))
            )
        return passed

    def send_cols():
        return [None] + [
            start(copy(inputs, col_in.at[:, :, col_at(z), :], iz_ss.at[d], iz_rs.at[d], me, col(d)))
            for d in range(1, m)
        ]

    def turn_cols():
        for o in range(p):
            for y in range(H):
                st_t[:, (o * H + y) * AZ : (o * H + y + 1) * AZ] = col_in[o, y].astype(F32).T.astype(BF16)
        whole_in[C : 2 * C, a_at(me, me)] = st_t[...]

    def mid(owner, target):
        return whole_in.at[pl.ds(C, C), a_at(owner, target)]

    def send_turned():
        direct = [None] + [
            start(copy(st_t, mid(me, to(t)), a_ss.at[1, t], a_rs.at[1, t], to(t), z))
            for t in range(1, nc)
        ]
        own = start(copy(st_t, mid(me, sib), af_ss.at[1, 0], af_rs.at[1, 0], sib, z))
        return direct, own

    def relay_turned(sent):
        direct, own = sent
        passed = [own]
        for t in range(1, nc):
            direct[t].wait_recv()
            d = frm(t)
            passed.append(
                start(copy(mid(d, me), mid(d, sib), af_ss.at[1, t], af_rs.at[1, t], sib, z))
            )
        return passed

    def roll_cols(first, last):
        def body(b, carry):
            at = pl.ds(pl.multiple_of(b * AZ, AZ), AZ)
            a = whole_in[C : 2 * C, at].astype(F32)
            whole_in[0:C, at] = pltpu.roll(a, 1, 1).astype(BF16)
            whole_in[2 * C : 3 * C, at] = pltpu.roll(a, AZ - 1, 1).astype(BF16)
            return carry

        lax.fori_loop(first, last, body, 0)

    def send_grad_cols():
        return [None] + [
            start(copy(st_g.at[1], home(1, me, chip, z), gz_ss.at[d], gz_rs.at[d], me, col(d)))
            for d in range(1, m)
        ]

    def spread_grad_cols(sent):
        forwards = []
        for k in range(1, m):
            sent[k].wait_recv()
            zz = col(m - k)
            here = home(1, me, chip, zz)
            passed = [start(copy(here, here, hf_ss.at[k, 0], hf_rs.at[k, 0], sib, z))]
            direct = [
                start(copy(here, home(1, me, there(t), zz), h_ss.at[k, t], h_rs.at[k, t], to(t), z))
                for t in range(1, nc)
            ]
            forwards.append((zz, passed, [None] + direct))
        return forwards

    def relay_grad_cols(forwards, ts):
        for k, (zz, passed, direct) in enumerate(forwards, 1):
            for t in ts:
                direct[t].wait_recv()
                here = home(1, frm(t), chip, zz)
                passed.append(start(copy(here, here, hf_ss.at[k, t], hf_rs.at[k, t], sib, z)))

    def group_terms(t, first, last):
        vs = list(range(2 * p * t, 2 * p * (t + 1)))
        if t == 0:
            vs = vs[p - 1 :]
        if last:
            vs = vs + list(range(p - 1))
        for i in range(3):
            low, high = max(0, i - 1), min(H, H + i - 1)
            left = jnp.concatenate(
                [whole_in[:, (v * H + low) * AZ : (v * H + high) * AZ] for v in vs], axis=1
            )
            count = (high - low) * AZ
            right = jnp.concatenate(
                [
                    jnp.concatenate(
                        [
                            whole_g[(v - s) % R, low + 1 - i : high + 1 - i].reshape(count, C)
                            for v in vs
                        ],
                        axis=0,
                    )
                    for s in range(p)
                ],
                axis=1,
            )
            got = jnp.dot(left, right, preferred_element_type=F32)
            if not first:
                got = got + acc[i]
            if not last:
                acc[i] = got
            else:
                for s in range(p):
                    for j in range(3):
                        out_f1[s, i, j] = got[j * C : (j + 1) * C, s * C : (s + 1) * C] * scale

    def arrive(copies):
        for c in copies:
            c.wait_recv()

    def build_gx(ph):
        x_of = lax.broadcasted_iota(jnp.int32, (p * H, X, C), 1).reshape(p * HX, C)

        def body(d, carry):
            g = grads[d] if ph == 0 else whole_g[g_at(d, chip), :, col_at(z), :]
            g = g.astype(F32).reshape(p * HX, C)
            low = edges[ph, d, 0].astype(F32)
            high = edges[ph, d, 1].astype(F32)
            low = jnp.broadcast_to(low[:, None, :], (p * H, X, C)).reshape(p * HX, C)
            high = jnp.broadcast_to(high[:, None, :], (p * H, X, C)).reshape(p * HX, C)
            before = jnp.where(x_of == 0, low, pltpu.roll(g, 1, 0))
            after = jnp.where(x_of == X - 1, high, pltpu.roll(g, p * HX - 1, 0))
            for j, v in enumerate((after, g, before)):
                gx[pl.ds(d * p, p), 1 : H + 1, :, j * C : (j + 1) * C] = v.astype(BF16).reshape(p, H, X, C)
            return carry

        lax.fori_loop(0, n, body, 0)

    def build_lhs():
        lane = lax.broadcasted_iota(jnp.int32, (C, HX), 1)
        for q in range(n):
            owner = lax.rem(me + q, n)
            for o in range(p):
                block = q * p + o
                a = feats[owner, o]
                wide = a.astype(F32)
                down = jnp.where(lane < X, 0.0, pltpu.roll(wide, X, 1)).astype(BF16)
                up = jnp.where(lane >= HX - X, 0.0, pltpu.roll(wide, HX - X, 1)).astype(BF16)
                spots = [block] + ([R + block] if block < p - 1 else [])
                for spot in spots:
                    for i, v in enumerate((down, a, up)):
                        lhs[i * C : (i + 1) * C, spot * HX : (spot + 1) * HX] = v

    def term(q, o):
        total = None
        for s in range(p):
            one = outs[(q * p + o - s) % R, :, s * C : (s + 1) * C]
            total = one if total is None else total + one
        return total

    def data_terms(ph):
        for load in loads[ph]:
            load.wait()
        w = weights[ph]
        crossed = [None] * n

        def emit(q):
            for o in range(p):
                part_s[ph, q, o] = term(q, o).astype(BF16)
            t = lax.rem(q // 2 + core, nc)
            crossed[q] = start(
                copy(part_s.at[ph, q], part_x.at[ph, t], x_ss.at[ph, t], x_rs.at[ph, t], sib, z)
            )

        for q in range(n):
            rows = jnp.concatenate(
                [gx[q * p : (q + 1) * p, 2 - i : 2 - i + H].reshape(p * HX, 3 * C) for i in range(3)],
                axis=1,
            )
            got = lax.dot_general(rows, w, (((1,), (1,)), ((), ())), preferred_element_type=F32)
            outs[q * p : (q + 1) * p] = got.reshape(p, HX, p * C)
            if q % 2 == 1:
                emit(q)

    def merge_terms(ph):
        sent = []
        for t in list(range(1, nc)) + [0]:
            pltpu.make_async_remote_copy(
                src_ref=part_x.at[ph, t], dst_ref=part_x.at[ph, t],
                send_sem=x_ss.at[ph, t], recv_sem=x_rs.at[ph, t],
                device_id={"rot": sib, "az": z}, device_id_type=pl.DeviceIdType.MESH,
            ).wait_recv()
            for o in range(p):
                total = term(2 * t, o) + part_x[ph, t, o].astype(F32)
                if t == 0:
                    part_r[ph, 0, o] = total.astype(BF16)
                else:
                    part_m[ph, t, o] = total.astype(BF16)
            if t > 0:
                sent.append(
                    start(
                        copy(part_m.at[ph, t], part_r.at[ph, t], p_ss.at[ph, t], p_rs.at[ph, t], to(t), z)
                    )
                )
        return sent

    def part_sum(ph, copies):
        arrive(copies)
        total = part_r[ph, 0].astype(F32)
        for t in range(1, nc):
            total = total + part_r[ph, t].astype(F32)
        return total

    lower = z < m // 2
    near_pos = jnp.where(lower, z, m - 1 - z)
    right, left = jnp.minimum(z + 1, m - 1), jnp.maximum(z - 1, 0)
    inner = jnp.where(lower, right, left)
    outer = jnp.where(lower, left, right)
    at_end = near_pos == 0
    at_mid = near_pos == m // 2 - 1
    slot = jnp.where(at_mid, 1, 0)

    def inward(src, k):
        return copy(src, zr.at[slot, k], z_ss.at[k], z_rs.at[slot, k], me, inner)

    def crossed_in(w, k):
        return copy(zr.at[w, k], zr.at[w, k], z_ss.at[k], z_rs.at[w, k], me, inner)

    def outward(k):
        return copy(zf.at[k], zf.at[k], y_ss.at[k], y_rs.at[k], me, outer)

    def filt_terms():
        right_side = gx[:, 1 : H + 1].reshape(R * HX, 3 * C)
        for s in range(p):
            got = jnp.dot(
                lhs[:, s * HX : (s + R) * HX], right_side, preferred_element_type=F32
            )
            for i in range(3):
                for j in range(3):
                    zs[(s * 3 + i) * 3 + j] = got[i * C : (i + 1) * C, j * C : (j + 1) * C].astype(BF16)
            begin(s * 18 // p, (s + 1) * 18 // p)

    def begin(a, b):
        @pl.when(at_end)
        def _():
            for k in range(K * a // 18, K * b // 18):
                inward(zs.at[k], k).start()

    def go_in(a, b):
        @pl.when(jnp.logical_not(at_end))
        def _():
            for k in range(K * a // 18, K * b // 18):
                crossed_in(0, k).wait_recv()
                zt[k] = (zs[k].astype(F32) + zr[0, k].astype(F32)).astype(BF16)
                inward(zt.at[k], k).start()

    base = zs if m == 2 else zt

    def go_out(a, b):
        for k in range(K * a // 18, K * b // 18):

            @pl.when(at_mid)
            def _():
                crossed_in(1, k).wait_recv()
                zf[k] = (base[k].astype(F32) + zr[1, k].astype(F32)).astype(BF16)

            @pl.when(jnp.logical_not(at_mid))
            def _():
                outward(k).wait_recv()

            @pl.when(jnp.logical_not(at_end))
            def _():
                outward(k).start()

            out_f2[k // 9, k // 3 % 3, k % 3] = zf[k].astype(F32) * scale

    def drain():
        for k in range(K):
            crossed_in(0, k).wait_send()

        @pl.when(jnp.logical_not(at_end))
        def _():
            for k in range(K):
                outward(k).wait_send()

    grad_two = (cot[...].astype(F32) * slope(pre_two[...].astype(F32))).astype(BF16).astype(F32)
    stage_grad(0, grad_two)
    col_in[:, :, col_at(z), :] = inputs[...]
    wide_one = pre_one[...].astype(F32)
    stage_feat((wide_one * jax.nn.sigmoid(wide_one)).reshape(p, HX, C))
    turn[...] = slope(wide_one)
    gx[:, 0] = jnp.zeros((R, X, 3 * C), BF16)
    gx[:, H + 1] = jnp.zeros((R, X, 3 * C), BF16)
    pl.semaphore_wait(barrier, len(partners))
    g_sent = send_grad(0)
    c_sent = send_cols()
    a_sent = send_feat()
    arrive(relay_grad(0, g_sent))
    build_gx(0)
    arrive(c_sent[1:])
    turn_cols()
    i_sent = send_turned()
    a_passed = relay_feat(a_sent)
    data_terms(0)
    p_sent = merge_terms(0)
    arrive(a_passed)
    build_lhs()
    filt_terms()

    delta = part_sum(0, p_sent).reshape(p, H, X, C)
    grad_one = (delta * turn[...]).astype(BF16).astype(F32)
    stage_grad(1, grad_one)
    g_sent = send_grad(1)
    z_sent = send_grad_cols()
    i_passed = relay_turned(i_sent)
    go_in(0, 2)
    arrive(i_passed)
    roll_cols(0, R * H)
    forwards = spread_grad_cols(z_sent)
    g_passed = relay_grad(1, g_sent)
    go_in(2, 6)
    arrive(g_passed)
    build_gx(1)
    go_in(6, 9)
    go_out(0, 3)
    data_terms(1)
    relay_grad_cols(forwards, range(1, nc))
    p_sent = merge_terms(1)
    go_in(9, 12)
    go_out(3, 7)
    for _, passed, _ in forwards:
        passed[0].wait_recv()
    group_terms(0, True, nc == 1)
    go_in(12, 18)
    go_out(7, 12)
    for t in range(1, nc):
        for _, passed, _ in forwards:
            passed[nc - t].wait_recv()
        group_terms(t, False, t == nc - 1)
        if t == 1:
            out_in[...] = part_sum(1, p_sent).astype(BF16).reshape(p, H, X, C)
    go_out(12, 18)
    for c in pending:
        c.wait_send()
    drain()


def solution(mesh):
    n, m = mesh.shape["rot"], mesh.shape["az"]

    def shards(inputs, pre_one, pre_two, cot, filt_one, filt_two):
        p, H, X, C = inputs.shape
        R, HX, K, nc = n * p, H * X, 9 * p, n // 2
        scale = float(R * H * X * m) ** -0.5
        dma = pltpu.SemaphoreType.DMA
        vmem = pl.BlockSpec(memory_space=pltpu.VMEM)
        AZ = X * m
        sums = jax.ShapeDtypeStruct((p, 3, 3, C, C), F32)
        return pl.pallas_call(
            functools.partial(kernel, n, m, p, H, X, C, scale),
            out_shape=(jax.ShapeDtypeStruct((p, H, X, C), BF16), sums, sums),
            in_specs=[vmem] * 4 + [pl.BlockSpec(memory_space=pl.ANY)] * 2,
            out_specs=(vmem,) * 3,
            scratch_shapes=[
                pltpu.VMEM((2, p, H, X, C), BF16),
                pltpu.VMEM((2, 2, p * H, C), BF16),
                pltpu.VMEM((p, C, HX), BF16),
                pltpu.VMEM((n, p, H, X, C), BF16),
                pltpu.VMEM((2, n, 2, p * H, C), BF16),
                pltpu.VMEM((n, p, C, HX), BF16),
                pltpu.VMEM((2, p * C, 9 * C), BF16),
                pltpu.VMEM((R, H + 2, X, 3 * C), BF16),
                pltpu.VMEM((3 * C, (R + p - 1) * HX), BF16),
                pltpu.VMEM((R, HX, p * C), F32),
                pltpu.VMEM((2, n, p, HX, C), BF16),
                pltpu.VMEM((2, nc, p, HX, C), BF16),
                pltpu.VMEM((2, nc, p, HX, C), BF16),
                pltpu.VMEM((2, nc, p, HX, C), BF16),
                pltpu.VMEM((K, C, C), BF16),
                pltpu.VMEM((2, K, C, C), BF16),
                pltpu.VMEM((K, C, C), BF16),
                pltpu.VMEM((K, C, C), BF16),
                pltpu.VMEM((p, H, AZ, C), BF16),
                pltpu.VMEM((C, p * H * AZ), BF16),
                pltpu.VMEM((3 * C, R * H * AZ), BF16),
                pltpu.VMEM((R, H, AZ, C), BF16),
                pltpu.VMEM((3, 3 * C, p * C), F32),
                pltpu.VMEM((p, H, X, C), F32),
            ]
            + [dma((2, nc))] * 4
            + [dma((2, 2, nc))] * 2
            + [dma((2, nc))] * 2
            + [dma((2, nc))] * 8
            + [dma((K,)), dma((2, K)), dma((K,)), dma((K,))]
            + [dma((2, K))]
            + [dma((m,))] * 4
            + [dma((m, nc))] * 4,
            compiler_params=pltpu.CompilerParams(
                collective_id=0, has_side_effects=True, vmem_limit_bytes=60 * 1024 * 1024
            ),
        )(inputs, pre_one, pre_two, cot, filt_one, filt_two)

    cells = P("rot", None, "az", None)
    banks = P("rot", None, None, None, None)
    return jax.shard_map(
        shards, mesh=mesh,
        in_specs=(cells,) * 4 + (banks,) * 2,
        out_specs=(cells, banks, banks),
        check_vma=False,
    )
```

time: 65.8 us -> 73.5 us (1.12)
  Pallas kernels: 61.4 us -> 67.6 us
  local copies, waits for them, and re-layouts: 0.63 us -> 4.97 us
  other arithmetic: 2.96 us -> 0 us
    pallas_call x1, Pallas kernels: 61.4 us -> 67.6 us  [shards(): pl.pallas_call(functools.partial(kernel, n, m, p, H, X, C, scale), out_sh...]
    unnamed x3 -> x5, local copies, waits for them, and re-layouts: 0.63 us -> 4.97 us
    mul x1 -> x0, other arithmetic: 2.96 us -> none  [widen(): return (v.astype(F32) * scale).reshape(p, 3, 3, C, C)]
where the time goes in v1:
time: 73.5 us; the launch traced here: 73.3 us
  Pallas kernels  67.6 us (92%)
  local copies, waits for them, and re-layouts  4.97 us (7%)
    pallas_call x1, Pallas kernels, shards(): pl.pallas_call(functools.partial(kernel, n, m, p, H, X, C, scale), out_sh...  67.6 us
    unnamed x5, local copies, waits for them, and re-layouts  4.97 us

profile of v1, /device:TPU:0, one launch (start us, length us, event | category | flops | bytes accessed | tf_op | source)
XLA Modules:
  0.0 73.3 jit_solution(9372275360708015007)
XLA Ops:
  0.6 67.6 %shard_map.85 = (bf16[2,4,32,128]{3,2,1,0:T(8,128)(2,1)}, f32[2,3,3,128,128]{4,3,2,1,0:T(8,128)}, f32[2,3,3,128,128]{4,3,2,1,0:T(8,128)}) custom-call(bf16[2,4,32,128]{3,2,1,0:T(8,128)(2,1)} %inputs.1, bf16[2,4,32,128]{3,2,1,0:T(8,128)(2,1)} %pre_one.1, bf16[2,4,32,128]{3,2,1,0:T(8,128)(2,1)} %pre_two.1, bf16[2,4,32,128]{3,2,1,0:T(8,128)(2,1)} %cot.1, ...), custom_call_target="tpu_custom_call" | custom-call | tf_op jit(solution)/shard_map/pallas_call | solution.py:526
  68.3 1.5 %copy.12 = bf16[2,4,32,128]{3,2,1,0:T(8,128)(2,1)} copy(bf16[2,4,32,128]{3,2,1,0:T(8,128)(2,1)} %get-tuple-element.6) | data formatting | bytes 131072
  69.8 0.0 copy-start
  69.8 2.5 %copy.13 = f32[2,3,3,128,128]{4,3,2,1,0:T(8,128)} copy(f32[2,3,3,128,128]{4,3,2,1,0:T(8,128)} %get-tuple-element.7) | data formatting | bytes 2359296
  72.2 0.0 copy-done
  72.2 1.0 %copy.14 = f32[2,3,3,128,128]{4,3,2,1,0:T(8,128)} copy(f32[2,3,3,128,128]{4,3,2,1,0:T(8,128)S(1)} %copy-done) | data formatting | bytes 2359296
Async XLA Ops:
  69.8 2.5 %copy-start = (f32[2,3,3,128,128]{4,3,2,1,0:T(8,128)S(1)}, f32[2,3,3,128,128]{4,3,2,1,0:T(8,128)}, u32[]{:S(2)}) copy-start(f32[2,3,3,128,128]{4,3,2,1,0:T(8,128)} %get-tuple-element.8) | copy-start | bytes 3538948

commit v2 on v1

--- a/solution.py
+++ b/solution.py
@@ -1,4 +1,5 @@
 import functools
+import math
 
 import jax
 import jax.numpy as jnp
@@ -18,21 +19,21 @@
 
 def kernel(
     n, m, p, H, X, C, scale,
-    inputs, pre_one, pre_two, cot, filt_one, filt_two,
+    inputs_at, pre_one_at, pre_two_at, cot_at, filt_one, filt_two,
     out_in, out_f1, out_f2,
+    inputs, pre_one, pre_two, cot, made_one, made_two,
     st_g, st_e, st_a, grads, edges, feats, weights, gx, lhs, outs,
     part_s, part_x, part_m, part_r, zs, zr, zt, zf,
-    col_in, st_t, whole_in, whole_g, acc, turn,
+    field_in, whole_in, whole_g, acc, turn,
     g_ss, g_rs, gf_ss, gf_rs, e_ss, e_rs, ef_ss, ef_rs, a_ss, a_rs, af_ss, af_rs,
     x_ss, x_rs, p_ss, p_rs, z_ss, z_rs, y_ss, y_rs,
-    w_sem, iz_ss, iz_rs, gz_ss, gz_rs, h_ss, h_rs, hf_ss, hf_rs,
+    w_sem, v_sem, o_sem, cz_ss, cz_rs, h_ss, h_rs, hf_ss, hf_rs,
 ):
     R = n * p
     HX = H * X
     nc = n // 2
     K = 9 * p
     AZ = m * X
-    span = p * H * AZ
     me = lax.axis_index("rot")
     z = lax.axis_index("az")
     core = lax.rem(me, 2)
@@ -56,13 +57,23 @@
 
     def a_at(owner, target):
         slot = lax.rem(owner - 2 * lax.div(target, 2) - target + 2 * n, n)
-        return pl.ds(pl.multiple_of(slot * span, span), span)
+        return pl.ds(p * slot, p)
 
     def copy(src, dst, ss, rs, rot, az):
         return pltpu.make_async_remote_copy(
             src_ref=src, dst_ref=dst, send_sem=ss, recv_sem=rs,
             device_id={"rot": rot, "az": az}, device_id_type=pl.DeviceIdType.MESH,
         )
+
+    lower = z < m // 2
+    near_pos = jnp.where(lower, z, m - 1 - z)
+    nearest = [sorted((c for c in range(m) if c != v), key=lambda c: (abs(c - v), c)) for v in range(m // 2)]
+
+    def other(k):
+        c = nearest[0][k]
+        for v in range(1, m // 2):
+            c = jnp.where(near_pos == v, nearest[v][k], c)
+        return jnp.where(lower, c, m - 1 - c)
 
     loads = [
         [
@@ -75,7 +86,14 @@
         ]
         for l, filt in enumerate((filt_two, filt_one))
     ]
-    for load in loads[0] + loads[1]:
+    fetch = [
+        pltpu.make_async_copy(a, b, v_sem.at[k])
+        for k, (a, b) in enumerate(
+            ((cot_at, cot), (pre_two_at, pre_two), (pre_one_at, pre_one), (inputs_at, inputs),
+             (inputs_at, field_in.at[a_at(me, me), :, col_at(z), :]))
+        )
+    ]
+    for load in fetch + loads[0] + loads[1]:
         load.start()
 
     barrier = pltpu.get_barrier_semaphore()
@@ -90,6 +108,12 @@
         )
 
     pending = []
+    leaving = []
+
+    def leave(made, out, f, k):
+        c = pltpu.make_async_copy(made.at[k], out.at[k], o_sem.at[f, k])
+        c.start()
+        leaving.append(c)
 
     def start(c):
         c.start()
@@ -175,76 +199,56 @@
             )
         return passed
 
-    def send_cols():
-        return [None] + [
-            start(copy(inputs, col_in.at[:, :, col_at(z), :], iz_ss.at[d], iz_rs.at[d], me, col(d)))
-            for d in range(1, m)
+    def source(f):
+        return st_g.at[1] if f else inputs
+
+    def place(f, owner, target, zz):
+        if f:
+            return whole_g.at[g_at(owner, lax.div(target, 2)), :, col_at(zz), :]
+        return field_in.at[a_at(owner, target), :, col_at(zz), :]
+
+    def send_cols(f):
+        return [
+            start(copy(source(f), place(f, me, me, z), cz_ss.at[f, k], cz_rs.at[f, z], me, other(k)))
+            for k in range(m - 1)
         ]
 
-    def turn_cols():
-        for o in range(p):
-            for y in range(H):
-                st_t[:, (o * H + y) * AZ : (o * H + y + 1) * AZ] = col_in[o, y].astype(F32).T.astype(BF16)
-        whole_in[C : 2 * C, a_at(me, me)] = st_t[...]
-
-    def mid(owner, target):
-        return whole_in.at[pl.ds(C, C), a_at(owner, target)]
-
-    def send_turned():
+    def spread_at(f, k, zz, src):
+        passed = [start(copy(src, place(f, me, sib, zz), hf_ss.at[f, k, 0], hf_rs.at[f, k, 0], sib, z))]
         direct = [None] + [
-            start(copy(st_t, mid(me, to(t)), a_ss.at[1, t], a_rs.at[1, t], to(t), z))
+            start(copy(src, place(f, me, to(t), zz), h_ss.at[f, k, t], h_rs.at[f, k, t], to(t), z))
             for t in range(1, nc)
         ]
-        own = start(copy(st_t, mid(me, sib), af_ss.at[1, 0], af_rs.at[1, 0], sib, z))
-        return direct, own
-
-    def relay_turned(sent):
-        direct, own = sent
-        passed = [own]
+        return zz, passed, direct
+
+    def spread_col(f, k):
+        zz = other(k)
+        here = place(f, me, me, zz)
+        copy(here, here, cz_ss.at[f, k], cz_rs.at[f, zz], me, zz).wait_recv()
+        return spread_at(f, k, zz, here)
+
+    def relay_cols(f, k, forward):
+        zz, passed, direct = forward
         for t in range(1, nc):
             direct[t].wait_recv()
             d = frm(t)
             passed.append(
-                start(copy(mid(d, me), mid(d, sib), af_ss.at[1, t], af_rs.at[1, t], sib, z))
-            )
-        return passed
-
-    def roll_cols(first, last):
-        def body(b, carry):
-            at = pl.ds(pl.multiple_of(b * AZ, AZ), AZ)
-            a = whole_in[C : 2 * C, at].astype(F32)
-            whole_in[0:C, at] = pltpu.roll(a, 1, 1).astype(BF16)
-            whole_in[2 * C : 3 * C, at] = pltpu.roll(a, AZ - 1, 1).astype(BF16)
+                start(
+                    copy(place(f, d, me, zz), place(f, d, sib, zz), hf_ss.at[f, k, t], hf_rs.at[f, k, t], sib, z)
+                )
+            )
+
+    def turn_group(t):
+        def body(v, carry):
+            for y in range(H):
+                at = pl.ds(pl.multiple_of((v * H + y) * AZ, AZ), AZ)
+                a = field_in[v, y].T
+                whole_in[C : 2 * C, at] = a
+                whole_in[0:C, at] = pltpu.roll(a, 1, 1)
+                whole_in[2 * C : 3 * C, at] = pltpu.roll(a, AZ - 1, 1)
             return carry
 
-        lax.fori_loop(first, last, body, 0)
-
-    def send_grad_cols():
-        return [None] + [
-            start(copy(st_g.at[1], home(1, me, chip, z), gz_ss.at[d], gz_rs.at[d], me, col(d)))
-            for d in range(1, m)
-        ]
-
-    def spread_grad_cols(sent):
-        forwards = []
-        for k in range(1, m):
-            sent[k].wait_recv()
-            zz = col(m - k)
-            here = home(1, me, chip, zz)
-            passed = [start(copy(here, here, hf_ss.at[k, 0], hf_rs.at[k, 0], sib, z))]
-            direct = [
-                start(copy(here, home(1, me, there(t), zz), h_ss.at[k, t], h_rs.at[k, t], to(t), z))
-                for t in range(1, nc)
-            ]
-            forwards.append((zz, passed, [None] + direct))
-        return forwards
-
-    def relay_grad_cols(forwards, ts):
-        for k, (zz, passed, direct) in enumerate(forwards, 1):
-            for t in ts:
-                direct[t].wait_recv()
-                here = home(1, frm(t), chip, zz)
-                passed.append(start(copy(here, here, hf_ss.at[k, t], hf_rs.at[k, t], sib, z)))
+        lax.fori_loop(2 * p * t, 2 * p * (t + 1), body, 0)
 
     def group_terms(t, first, last):
         vs = list(range(2 * p * t, 2 * p * (t + 1)))
@@ -279,7 +283,9 @@
             else:
                 for s in range(p):
                     for j in range(3):
-                        out_f1[s, i, j] = got[j * C : (j + 1) * C, s * C : (s + 1) * C] * scale
+                        k = (s * 3 + i) * 3 + j
+                        made_one[k] = got[j * C : (j + 1) * C, s * C : (s + 1) * C] * scale
+                        leave(made_one, out_f1, 0, k)
 
     def arrive(copies):
         for c in copies:
@@ -325,7 +331,7 @@
             total = one if total is None else total + one
         return total
 
-    def data_terms(ph):
+    def data_terms(ph, beside):
         for load in loads[ph]:
             load.wait()
         w = weights[ph]
@@ -348,6 +354,8 @@
             outs[q * p : (q + 1) * p] = got.reshape(p, HX, p * C)
             if q % 2 == 1:
                 emit(q)
+            if q in beside:
+                beside[q]()
 
     def merge_terms(ph):
         sent = []
@@ -378,8 +386,6 @@
             total = total + part_r[ph, t].astype(F32)
         return total
 
-    lower = z < m // 2
-    near_pos = jnp.where(lower, z, m - 1 - z)
     right, left = jnp.minimum(z + 1, m - 1), jnp.maximum(z - 1, 0)
     inner = jnp.where(lower, right, left)
     outer = jnp.where(lower, left, right)
@@ -405,7 +411,8 @@
             for i in range(3):
                 for j in range(3):
                     zs[(s * 3 + i) * 3 + j] = got[i * C : (i + 1) * C, j * C : (j + 1) * C].astype(BF16)
-            begin(s * 18 // p, (s + 1) * 18 // p)
+            if s == 0:
+                begin(0, min(7, 18 // p))
 
     def begin(a, b):
         @pl.when(at_end)
@@ -423,23 +430,30 @@
 
     base = zs if m == 2 else zt
 
-    def go_out(a, b):
-        for k in range(K * a // 18, K * b // 18):
-
-            @pl.when(at_mid)
-            def _():
+    def cross(a, b):
+        @pl.when(at_mid)
+        def _():
+            for k in range(K * a // 18, K * b // 18):
                 crossed_in(1, k).wait_recv()
                 zf[k] = (base[k].astype(F32) + zr[1, k].astype(F32)).astype(BF16)
+
+                @pl.when(jnp.logical_not(at_end))
+                def _():
+                    outward(k).start()
+
+    def settle(a, b):
+        for k in range(K * a // 18, K * b // 18):
 
             @pl.when(jnp.logical_not(at_mid))
             def _():
                 outward(k).wait_recv()
 
-            @pl.when(jnp.logical_not(at_end))
-            def _():
-                outward(k).start()
-
-            out_f2[k // 9, k // 3 % 3, k % 3] = zf[k].astype(F32) * scale
+                @pl.when(jnp.logical_not(at_end))
+                def _():
+                    outward(k).start()
+
+            made_two[k] = zf[k].astype(F32) * scale
+            leave(made_two, out_f2, 1, k)
 
     def drain():
         for k in range(K):
@@ -450,66 +464,109 @@
             for k in range(K):
                 outward(k).wait_send()
 
+    fetch[0].wait()
+    fetch[1].wait()
     grad_two = (cot[...].astype(F32) * slope(pre_two[...].astype(F32))).astype(BF16).astype(F32)
     stage_grad(0, grad_two)
-    col_in[:, :, col_at(z), :] = inputs[...]
+    fetch[2].wait()
     wide_one = pre_one[...].astype(F32)
     stage_feat((wide_one * jax.nn.sigmoid(wide_one)).reshape(p, HX, C))
     turn[...] = slope(wide_one)
     gx[:, 0] = jnp.zeros((R, X, 3 * C), BF16)
     gx[:, H + 1] = jnp.zeros((R, X, 3 * C), BF16)
+    fetch[3].wait()
+    fetch[4].wait()
     pl.semaphore_wait(barrier, len(partners))
     g_sent = send_grad(0)
-    c_sent = send_cols()
+    send_cols(0)
     a_sent = send_feat()
-    arrive(relay_grad(0, g_sent))
+    moves = {(0, m - 1): spread_at(0, m - 1, z, inputs)}
+
+    def spread(f, *ks):
+        for k in ks:
+            if k < m - 1:
+                moves[f, k] = spread_col(f, k)
+
+    def relay(f, *ks):
+        for k in ks:
+            relay_cols(f, k, moves[f, k])
+
+    kept = {}
+    g_passed = relay_grad(0, g_sent)
+    spread(0, 0)
+    arrive(g_passed)
     build_gx(0)
-    arrive(c_sent[1:])
-    turn_cols()
-    i_sent = send_turned()
-    a_passed = relay_feat(a_sent)
-    data_terms(0)
+    data_terms(0, {
+        n // 8: lambda: spread(0, 1),
+        n // 2: lambda: kept.update(a=relay_feat(a_sent)),
+    })
+    arrive(kept["a"])
+    build_lhs()
     p_sent = merge_terms(0)
-    arrive(a_passed)
-    build_lhs()
+    spread(0, *range(2, m - 1))
     filt_terms()
+    relay(0, m - 1, *range(min(2, m - 1)))
 
     delta = part_sum(0, p_sent).reshape(p, H, X, C)
     grad_one = (delta * turn[...]).astype(BF16).astype(F32)
     stage_grad(1, grad_one)
     g_sent = send_grad(1)
-    z_sent = send_grad_cols()
-    i_passed = relay_turned(i_sent)
-    go_in(0, 2)
-    arrive(i_passed)
-    roll_cols(0, R * H)
-    forwards = spread_grad_cols(z_sent)
+    send_cols(1)
+    begin(min(7, 18 // p), 18)
+    relay(0, *range(2, m - 1))
+    go_in(0, 7)
+    for k in range(m):
+        arrive(moves[0, k][1])
+    half = nc // 2
+    for t in range(half):
+        turn_group(t)
+    spread(1, 0)
     g_passed = relay_grad(1, g_sent)
-    go_in(2, 6)
     arrive(g_passed)
     build_gx(1)
-    go_in(6, 9)
-    go_out(0, 3)
-    data_terms(1)
-    relay_grad_cols(forwards, range(1, nc))
+    data_terms(1, {
+        n // 4: lambda: spread(1, 1),
+        3 * n // 4: lambda: spread(1, *range(2, m - 1)),
+    })
+    go_in(7, 11)
     p_sent = merge_terms(1)
-    go_in(9, 12)
-    go_out(3, 7)
-    for _, passed, _ in forwards:
+    for t in range(half, nc):
+        turn_group(t)
+    relay(1, *range(min(2, m - 1)))
+    go_in(11, 18)
+    cross(0, 7)
+    relay(1, *range(2, m - 1))
+    cols = [moves[1, k][1] for k in range(m - 1)]
+    for passed in cols:
         passed[0].wait_recv()
     group_terms(0, True, nc == 1)
-    go_in(12, 18)
-    go_out(7, 12)
+    settle(0, 7)
+    cross(7, 11)
+    out_in[...] = part_sum(1, p_sent).astype(BF16).reshape(p, H, X, C)
     for t in range(1, nc):
-        for _, passed, _ in forwards:
+        for passed in cols:
             passed[nc - t].wait_recv()
         group_terms(t, False, t == nc - 1)
         if t == 1:
-            out_in[...] = part_sum(1, p_sent).astype(BF16).reshape(p, H, X, C)
-    go_out(12, 18)
+            settle(7, 11)
+            cross(11, 18)
+    settle(11, 18)
     for c in pending:
         c.wait_send()
     drain()
+    for c in leaving:
+        c.wait()
+
+
+def emit(got, sum_one, sum_two, out, out_one, out_two, sems):
+    moves = [
+        pltpu.make_async_copy(a, b, sems.at[k])
+        for k, (a, b) in enumerate(((sum_one, out_one), (sum_two, out_two), (got, out)))
+    ]
+    for c in moves:
+        c.start()
+    for c in moves:
+        c.wait()
 
 
 def solution(mesh):
@@ -522,50 +579,68 @@
         dma = pltpu.SemaphoreType.DMA
         vmem = pl.BlockSpec(memory_space=pltpu.VMEM)
         AZ = X * m
-        sums = jax.ShapeDtypeStruct((p, 3, 3, C, C), F32)
-        return pl.pallas_call(
+        anywhere = pl.BlockSpec(memory_space=pl.ANY)
+        sums = jax.ShapeDtypeStruct((K, C, C), F32)
+        scratch = [
+            pltpu.VMEM((p, H, X, C), BF16),
+            pltpu.VMEM((p, H, X, C), BF16),
+            pltpu.VMEM((p, H, X, C), BF16),
+            pltpu.VMEM((p, H, X, C), BF16),
+            pltpu.VMEM((K, C, C), F32),
+            pltpu.VMEM((K, C, C), F32),
+        pltpu.VMEM((2, p, H, X, C), BF16),
+        pltpu.VMEM((2, 2, p * H, C), BF16),
+        pltpu.VMEM((p, C, HX), BF16),
+        pltpu.VMEM((n, p, H, X, C), BF16),
+        pltpu.VMEM((2, n, 2, p * H, C), BF16),
+        pltpu.VMEM((n, p, C, HX), BF16),
+        pltpu.VMEM((2, p * C, 9 * C), BF16),
+        pltpu.VMEM((R, H + 2, X, 3 * C), BF16),
+        pltpu.VMEM((3 * C, (R + p - 1) * HX), BF16),
+        pltpu.VMEM((R, HX, p * C), F32),
+        pltpu.VMEM((2, n, p, HX, C), BF16),
+        pltpu.VMEM((2, nc, p, HX, C), BF16),
+        pltpu.VMEM((2, nc, p, HX, C), BF16),
+        pltpu.VMEM((2, nc, p, HX, C), BF16),
+        pltpu.VMEM((K, C, C), BF16),
+        pltpu.VMEM((2, K, C, C), BF16),
+        pltpu.VMEM((K, C, C), BF16),
+        pltpu.VMEM((K, C, C), BF16),
+        pltpu.VMEM((R, H, AZ, C), BF16),
+        pltpu.VMEM((3 * C, R * H * AZ), BF16),
+        pltpu.VMEM((R, H, AZ, C), BF16),
+        pltpu.VMEM((3, 3 * C, p * C), F32),
+        pltpu.VMEM((p, H, X, C), F32),
+        ]
+        held = sum(math.prod(v.shape) * jnp.dtype(v.dtype).itemsize for v in scratch)
+        held += 2 * inputs.size
+        made = pl.pallas_call(
             functools.partial(kernel, n, m, p, H, X, C, scale),
             out_shape=(jax.ShapeDtypeStruct((p, H, X, C), BF16), sums, sums),
-            in_specs=[vmem] * 4 + [pl.BlockSpec(memory_space=pl.ANY)] * 2,
-            out_specs=(vmem,) * 3,
-            scratch_shapes=[
-                pltpu.VMEM((2, p, H, X, C), BF16),
-                pltpu.VMEM((2, 2, p * H, C), BF16),
-                pltpu.VMEM((p, C, HX), BF16),
-                pltpu.VMEM((n, p, H, X, C), BF16),
-                pltpu.VMEM((2, n, 2, p * H, C), BF16),
-                pltpu.VMEM((n, p, C, HX), BF16),
-                pltpu.VMEM((2, p * C, 9 * C), BF16),
-                pltpu.VMEM((R, H + 2, X, 3 * C), BF16),
-                pltpu.VMEM((3 * C, (R + p - 1) * HX), BF16),
-                pltpu.VMEM((R, HX, p * C), F32),
-                pltpu.VMEM((2, n, p, HX, C), BF16),
-                pltpu.VMEM((2, nc, p, HX, C), BF16),
-                pltpu.VMEM((2, nc, p, HX, C), BF16),
-                pltpu.VMEM((2, nc, p, HX, C), BF16),
-                pltpu.VMEM((K, C, C), BF16),
-                pltpu.VMEM((2, K, C, C), BF16),
-                pltpu.VMEM((K, C, C), BF16),
-                pltpu.VMEM((K, C, C), BF16),
-                pltpu.VMEM((p, H, AZ, C), BF16),
-                pltpu.VMEM((C, p * H * AZ), BF16),
-                pltpu.VMEM((3 * C, R * H * AZ), BF16),
-                pltpu.VMEM((R, H, AZ, C), BF16),
-                pltpu.VMEM((3, 3 * C, p * C), F32),
-                pltpu.VMEM((p, H, X, C), F32),
-            ]
+            in_specs=[pl.BlockSpec(memory_space=pltpu.HBM)] * 6,
+            out_specs=(vmem, anywhere, anywhere),
+            scratch_shapes=scratch
             + [dma((2, nc))] * 4
             + [dma((2, 2, nc))] * 2
             + [dma((2, nc))] * 2
             + [dma((2, nc))] * 8
             + [dma((K,)), dma((2, K)), dma((K,)), dma((K,))]
-            + [dma((2, K))]
-            + [dma((m,))] * 4
-            + [dma((m, nc))] * 4,
+            + [dma((2, K)), dma((5,)), dma((2, K))]
+            + [dma((2, m))] * 2
+            + [dma((2, m, nc))] * 4,
             compiler_params=pltpu.CompilerParams(
-                collective_id=0, has_side_effects=True, vmem_limit_bytes=60 * 1024 * 1024
+                collective_id=0, has_side_effects=True, vmem_limit_bytes=held + 3 * 1024 * 1024
             ),
-        )(inputs, pre_one, pre_two, cot, filt_one, filt_two)
+        )(*(pltpu.with_memory_space_constraint(v, pltpu.HBM) for v in (inputs, pre_one, pre_two, cot, filt_one, filt_two)))
+        got, one, two = pl.pallas_call(
+            emit,
+            out_shape=tuple(jax.ShapeDtypeStruct(v.shape, v.dtype) for v in made),
+            in_specs=[vmem] * 3,
+            out_specs=(anywhere,) * 3,
+            scratch_shapes=[dma((3,))],
+            compiler_params=pltpu.CompilerParams(vmem_limit_bytes=4 * 1024 * 1024),
+        )(*made)
+        return got, one.reshape(p, 3, 3, C, C), two.reshape(p, 3, 3, C, C)
 
     cells = P("rot", None, "az", None)
     banks = P("rot", None, None, None, None)

time: 73.5 us -> 63.5 us (0.86)
  Pallas kernels: 67.6 us -> 62.5 us
  local copies, waits for them, and re-layouts: 4.97 us -> 0 us
    pallas_call x1, Pallas kernels: 67.6 us -> 61.1 us  [shards(): pl.pallas_call(functools.partial(kernel, n, m, p, H, X, C, scale), out_sh...]
    unnamed x5 -> x0, local copies, waits for them, and re-layouts: 4.97 us -> none
    pallas_call x0 -> x1, Pallas kernels: none -> 1.43 us  [shards(): pl.pallas_call(emit, out_shape=tuple((jax.ShapeDtypeStruct(v.shape, v.dty...]
where the time goes in v2:
time: 63.5 us; the launch traced here: 63.3 us
  Pallas kernels  62.5 us (98%)
  between operations  0.8 us (1%)
    pallas_call x1, Pallas kernels, shards(): pl.pallas_call(functools.partial(kernel, n, m, p, H, X, C, scale), out_sh...  61.1 us
    pallas_call x1, Pallas kernels, shards(): pl.pallas_call(emit, out_shape=tuple((jax.ShapeDtypeStruct(v.shape, v.dty...  1.43 us

profile of v2, /device:TPU:0, one launch (start us, length us, event | category | flops | bytes accessed | tf_op | source)
XLA Modules:
  0.0 63.3 jit_solution(682326515180609813)
XLA Ops:
  0.6 61.1 %shard_map.85 = (bf16[2,4,32,128]{3,2,1,0:T(8,128)(2,1)S(1)}, f32[18,128,128]{2,1,0:T(8,128)S(1)}, f32[18,128,128]{2,1,0:T(8,128)S(1)}) custom-call(bf16[2,4,32,128]{3,2,1,0:T(8,128)(2,1)} %inputs_at.1, bf16[2,4,32,128]{3,2,1,0:T(8,128)(2,1)} %pre_one_at.1, bf16[2,4,32,128]{3,2,1,0:T(8,128)(2,1)} %pre_two_at.1, bf16[2,4,32,128]{3,2,1,0:T(8,128)(2,1)} %cot_at.1, ...), custom_call_target="tpu_custom_call" | custom-call | tf_op jit(solution)/shard_map/pallas_call | solution.py:617
  61.7 1.4 %shard_map.86 = (bf16[2,4,32,128]{3,2,1,0:T(8,128)(2,1)}, f32[18,128,128]{2,1,0:T(8,128)}, f32[18,128,128]{2,1,0:T(8,128)}) custom-call(bf16[2,4,32,128]{3,2,1,0:T(8,128)(2,1)S(1)} %get-tuple-element.9.got, f32[18,128,128]{2,1,0:T(8,128)S(1)} %get-tuple-element.10.sum_one, f32[18,128,128]{2,1,0:T(8,128)S(1)} %get-tuple-element.11.sum_two), custom_call_target="tpu_custom_call" | custom-call | tf_op jit(solution)/shard_map/pallas_call | solution.py:635

commit v3 on v2

--- a/solution.py
+++ b/solution.py
@@ -18,22 +18,21 @@
 
 
 def kernel(
-    n, m, p, H, X, C, scale,
+    n, m, p, H, X, C,
     inputs_at, pre_one_at, pre_two_at, cot_at, filt_one, filt_two,
     out_in, out_f1, out_f2,
-    inputs, pre_one, pre_two, cot, made_one, made_two,
+    inputs, pre_one, pre_two, cot,
     st_g, st_e, st_a, grads, edges, feats, weights, gx, lhs, outs,
-    part_s, part_x, part_m, part_r, zs, zr, zt, zf,
+    part_s, part_x, part_m, part_r, zs, zr, zt,
     field_in, whole_in, whole_g, acc, turn,
     g_ss, g_rs, gf_ss, gf_rs, e_ss, e_rs, ef_ss, ef_rs, a_ss, a_rs, af_ss, af_rs,
     x_ss, x_rs, p_ss, p_rs, z_ss, z_rs, y_ss, y_rs,
-    w_sem, v_sem, o_sem, cz_ss, cz_rs, h_ss, h_rs, hf_ss, hf_rs,
+    w_sem, v_sem, cz_ss, cz_rs, h_ss, h_rs, hf_ss, hf_rs,
 ):
     R = n * p
     HX = H * X
     nc = n // 2
     K = 9 * p
-    AZ = m * X
     me = lax.axis_index("rot")
     z = lax.axis_index("az")
     core = lax.rem(me, 2)
@@ -48,9 +47,6 @@
 
     def col(d):
         return lax.rem(z + d, m)
-
-    def col_at(zz):
-        return pl.ds(pl.multiple_of(zz * X, X), X)
 
     def g_at(owner, target_chip):
         return pl.ds(p * lax.rem(owner - 2 * target_chip + n, n), p)
@@ -90,7 +86,7 @@
         pltpu.make_async_copy(a, b, v_sem.at[k])
         for k, (a, b) in enumerate(
             ((cot_at, cot), (pre_two_at, pre_two), (pre_one_at, pre_one), (inputs_at, inputs),
-             (inputs_at, field_in.at[a_at(me, me), :, col_at(z), :]))
+             (inputs_at, field_in.at[a_at(me, me), z]))
         )
     ]
     for load in fetch + loads[0] + loads[1]:
@@ -108,13 +104,6 @@
         )
 
     pending = []
-    leaving = []
-
-    def leave(made, out, f, k):
-        c = pltpu.make_async_copy(made.at[k], out.at[k], o_sem.at[f, k])
-        c.start()
-        leaving.append(c)
-
     def start(c):
         c.start()
         pending.append(c)
@@ -125,14 +114,14 @@
         if ph == 0:
             grads[me] = value.astype(BF16)
         else:
-            whole_g[g_at(me, chip), :, col_at(z), :] = value.astype(BF16)
+            whole_g[g_at(me, chip), z, 1 : H + 1] = value.astype(BF16)
         st_e[ph, 0] = value[:, :, 0, :].reshape(p * H, C).astype(BF16)
         st_e[ph, 1] = value[:, :, X - 1, :].reshape(p * H, C).astype(BF16)
 
     def home(ph, owner, target_chip, zz):
         if ph == 0:
             return grads.at[owner]
-        return whole_g.at[g_at(owner, target_chip), :, col_at(zz), :]
+        return whole_g.at[g_at(owner, target_chip), zz, pl.ds(1, H)]
 
     def there(t):
         return lax.rem(chip + t, nc)
@@ -204,8 +193,8 @@
 
     def place(f, owner, target, zz):
         if f:
-            return whole_g.at[g_at(owner, lax.div(target, 2)), :, col_at(zz), :]
-        return field_in.at[a_at(owner, target), :, col_at(zz), :]
+            return home(1, owner, lax.div(target, 2), zz)
+        return field_in.at[a_at(owner, target), zz]
 
     def send_cols(f):
         return [
@@ -238,54 +227,57 @@
                 )
             )
 
-    def turn_group(t):
-        def body(v, carry):
-            for y in range(H):
-                at = pl.ds(pl.multiple_of((v * H + y) * AZ, AZ), AZ)
-                a = field_in[v, y].T
-                whole_in[C : 2 * C, at] = a
-                whole_in[0:C, at] = pltpu.roll(a, 1, 1)
-                whole_in[2 * C : 3 * C, at] = pltpu.roll(a, AZ - 1, 1)
+    def turn_col(zz):
+        x_of = lax.broadcasted_iota(jnp.int32, (H, X, C), 1).reshape(HX, C)
+        many = 4 if R % 4 == 0 else 1
+
+        def rim(v, c, x):
+            edge = field_in[v, c].astype(F32)[:, x, :]
+            return jnp.broadcast_to(edge[:, None, :], (H, X, C)).reshape(HX, C)
+
+        def body(b, carry):
+            for u in range(many):
+                v = b * many + u
+                at = pl.ds(pl.multiple_of((zz * R + v) * HX, HX), HX)
+                a = field_in[v, zz].reshape(HX, C)
+                wide = a.astype(F32)
+                low = rim(v, lax.rem(zz + m - 1, m), X - 1)
+                high = rim(v, lax.rem(zz + 1, m), 0)
+                before = jnp.where(x_of == 0, low, pltpu.roll(wide, 1, 0))
+                after = jnp.where(x_of == X - 1, high, pltpu.roll(wide, HX - 1, 0))
+                whole_in[0:C, at] = before.astype(BF16).T
+                whole_in[C : 2 * C, at] = a.T
+                whole_in[2 * C : 3 * C, at] = after.astype(BF16).T
             return carry
 
-        lax.fori_loop(2 * p * t, 2 * p * (t + 1), body, 0)
-
-    def group_terms(t, first, last):
-        vs = list(range(2 * p * t, 2 * p * (t + 1)))
-        if t == 0:
-            vs = vs[p - 1 :]
-        if last:
-            vs = vs + list(range(p - 1))
+        lax.fori_loop(0, R // many, body, 0)
+
+    def column(step):
+        if m != 4:
+            return step
+        return z if step == 0 else other(step - 1)
+
+    def col_terms(step):
+        zz = column(step)
         for i in range(3):
-            low, high = max(0, i - 1), min(H, H + i - 1)
-            left = jnp.concatenate(
-                [whole_in[:, (v * H + low) * AZ : (v * H + high) * AZ] for v in vs], axis=1
-            )
-            count = (high - low) * AZ
-            right = jnp.concatenate(
-                [
-                    jnp.concatenate(
-                        [
-                            whole_g[(v - s) % R, low + 1 - i : high + 1 - i].reshape(count, C)
-                            for v in vs
-                        ],
-                        axis=0,
-                    )
-                    for s in range(p)
-                ],
-                axis=1,
-            )
-            got = jnp.dot(left, right, preferred_element_type=F32)
-            if not first:
-                got = got + acc[i]
-            if not last:
-                acc[i] = got
-            else:
+            left = whole_in[:, pl.ds(pl.multiple_of(zz * R * HX, R * HX), R * HX)]
+            sides = []
+            for s in range(p):
+                rows = [whole_g[R - s : R, zz, 2 - i : 2 - i + H].reshape(s * HX, C)] if s else []
+                rows.append(whole_g[0 : R - s, zz, 2 - i : 2 - i + H].reshape((R - s) * HX, C))
+                sides.append(jnp.concatenate(rows, axis=0))
+            got = jnp.dot(left, jnp.concatenate(sides, axis=1), preferred_element_type=F32)
+            if step == m - 1:
+                if m == 4:
+                    got = got + acc[1, i]
+                got = got + acc[0, i]
                 for s in range(p):
                     for j in range(3):
-                        k = (s * 3 + i) * 3 + j
-                        made_one[k] = got[j * C : (j + 1) * C, s * C : (s + 1) * C] * scale
-                        leave(made_one, out_f1, 0, k)
+                        out_f1[(s * 3 + i) * 3 + j] = got[j * C : (j + 1) * C, s * C : (s + 1) * C].astype(BF16)
+            elif step == 0 or (m == 4 and step == 2):
+                acc[step // 2, i] = got
+            else:
+                acc[0, i] = acc[0, i] + got
 
     def arrive(copies):
         for c in copies:
@@ -295,7 +287,7 @@
         x_of = lax.broadcasted_iota(jnp.int32, (p * H, X, C), 1).reshape(p * HX, C)
 
         def body(d, carry):
-            g = grads[d] if ph == 0 else whole_g[g_at(d, chip), :, col_at(z), :]
+            g = grads[d] if ph == 0 else whole_g[g_at(d, chip), z, 1 : H + 1]
             g = g.astype(F32).reshape(p * HX, C)
             low = edges[ph, d, 0].astype(F32)
             high = edges[ph, d, 1].astype(F32)
@@ -400,7 +392,7 @@
         return copy(zr.at[w, k], zr.at[w, k], z_ss.at[k], z_rs.at[w, k], me, inner)
 
     def outward(k):
-        return copy(zf.at[k], zf.at[k], y_ss.at[k], y_rs.at[k], me, outer)
+        return copy(out_f2.at[k], out_f2.at[k], y_ss.at[k], y_rs.at[k], me, outer)
 
     def filt_terms():
         right_side = gx[:, 1 : H + 1].reshape(R * HX, 3 * C)
@@ -435,7 +427,7 @@
         def _():
             for k in range(K * a // 18, K * b // 18):
                 crossed_in(1, k).wait_recv()
-                zf[k] = (base[k].astype(F32) + zr[1, k].astype(F32)).astype(BF16)
+                out_f2[k] = (base[k].astype(F32) + zr[1, k].astype(F32)).astype(BF16)
 
                 @pl.when(jnp.logical_not(at_end))
                 def _():
@@ -452,8 +444,6 @@
                 def _():
                     outward(k).start()
 
-            made_two[k] = zf[k].astype(F32) * scale
-            leave(made_two, out_f2, 1, k)
 
     def drain():
         for k in range(K):
@@ -474,6 +464,8 @@
     turn[...] = slope(wide_one)
     gx[:, 0] = jnp.zeros((R, X, 3 * C), BF16)
     gx[:, H + 1] = jnp.zeros((R, X, 3 * C), BF16)
+    whole_g[:, :, 0] = jnp.zeros((R, m, X, C), BF16)
+    whole_g[:, :, H + 1] = jnp.zeros((R, m, X, C), BF16)
     fetch[3].wait()
     fetch[4].wait()
     pl.semaphore_wait(barrier, len(partners))
@@ -517,11 +509,16 @@
     go_in(0, 7)
     for k in range(m):
         arrive(moves[0, k][1])
-    half = nc // 2
-    for t in range(half):
-        turn_group(t)
+    if m != 4:
+        for c in range(m):
+            turn_col(c)
+    else:
+        turn_col(column(0))
+        turn_col(column(1))
     spread(1, 0)
     g_passed = relay_grad(1, g_sent)
+    if m == 4:
+        turn_col(column(2))
     arrive(g_passed)
     build_gx(1)
     data_terms(1, {
@@ -530,41 +527,52 @@
     })
     go_in(7, 11)
     p_sent = merge_terms(1)
-    for t in range(half, nc):
-        turn_group(t)
-    relay(1, *range(min(2, m - 1)))
+    cols = [moves[1, k][1] for k in range(m - 1)]
+    if m == 4:
+        turn_col(column(3))
+        col_terms(0)
+    relay(1, 0)
     go_in(11, 18)
     cross(0, 7)
-    relay(1, *range(2, m - 1))
-    cols = [moves[1, k][1] for k in range(m - 1)]
-    for passed in cols:
-        passed[0].wait_recv()
-    group_terms(0, True, nc == 1)
+    relay(1, *range(1, m - 1))
+    if m == 4:
+        arrive(cols[0])
+        col_terms(1)
     settle(0, 7)
     cross(7, 11)
     out_in[...] = part_sum(1, p_sent).astype(BF16).reshape(p, H, X, C)
-    for t in range(1, nc):
+    if m == 4:
+        arrive(cols[1])
+        col_terms(2)
+    settle(7, 11)
+    cross(11, 18)
+    if m == 4:
+        arrive(cols[2])
+        col_terms(3)
+    else:
         for passed in cols:
-            passed[nc - t].wait_recv()
-        group_terms(t, False, t == nc - 1)
-        if t == 1:
-            settle(7, 11)
-            cross(11, 18)
+            arrive(passed)
+        for step in range(m):
+            col_terms(step)
     settle(11, 18)
     for c in pending:
         c.wait_send()
     drain()
-    for c in leaving:
-        c.wait()
-
-
-def emit(got, sum_one, sum_two, out, out_one, out_two, sems):
-    moves = [
-        pltpu.make_async_copy(a, b, sems.at[k])
-        for k, (a, b) in enumerate(((sum_one, out_one), (sum_two, out_two), (got, out)))
-    ]
-    for c in moves:
-        c.start()
+
+
+def emit(scale, got, one, two, out, out_one, out_two, wide, sems):
+    k, half = one.shape[0], one.shape[0] // 3
+    moves = [pltpu.make_async_copy(got, out, sems.at[0])]
+    moves[0].start()
+    for f, (a, b) in enumerate(((one, out_one), (two, out_two))):
+        for c in range(0, k, half):
+            wide[f, c : c + half] = a[c : c + half].astype(F32) * scale
+            moves.append(
+                pltpu.make_async_copy(
+                    wide.at[f, c : c + half], b.at[c : c + half], sems.at[1 + f * 3 + c // half]
+                )
+            )
+            moves[-1].start()
     for c in moves:
         c.wait()
 
@@ -578,16 +586,13 @@
         scale = float(R * H * X * m) ** -0.5
         dma = pltpu.SemaphoreType.DMA
         vmem = pl.BlockSpec(memory_space=pltpu.VMEM)
-        AZ = X * m
         anywhere = pl.BlockSpec(memory_space=pl.ANY)
-        sums = jax.ShapeDtypeStruct((K, C, C), F32)
+        sums = jax.ShapeDtypeStruct((K, C, C), BF16)
         scratch = [
             pltpu.VMEM((p, H, X, C), BF16),
             pltpu.VMEM((p, H, X, C), BF16),
             pltpu.VMEM((p, H, X, C), BF16),
             pltpu.VMEM((p, H, X, C), BF16),
-            pltpu.VMEM((K, C, C), F32),
-            pltpu.VMEM((K, C, C), F32),
         pltpu.VMEM((2, p, H, X, C), BF16),
         pltpu.VMEM((2, 2, p * H, C), BF16),
         pltpu.VMEM((p, C, HX), BF16),
@@ -605,27 +610,26 @@
         pltpu.VMEM((K, C, C), BF16),
         pltpu.VMEM((2, K, C, C), BF16),
         pltpu.VMEM((K, C, C), BF16),
-        pltpu.VMEM((K, C, C), BF16),
-        pltpu.VMEM((R, H, AZ, C), BF16),
-        pltpu.VMEM((3 * C, R * H * AZ), BF16),
-        pltpu.VMEM((R, H, AZ, C), BF16),
-        pltpu.VMEM((3, 3 * C, p * C), F32),
+        pltpu.VMEM((R, m, H, X, C), BF16),
+        pltpu.VMEM((3 * C, m * R * HX), BF16),
+        pltpu.VMEM((R, m, H + 2, X, C), BF16),
+        pltpu.VMEM((2, 3, 3 * C, p * C), F32),
         pltpu.VMEM((p, H, X, C), F32),
         ]
         held = sum(math.prod(v.shape) * jnp.dtype(v.dtype).itemsize for v in scratch)
-        held += 2 * inputs.size
+        held += 2 * inputs.size + 2 * 2 * K * C * C
         made = pl.pallas_call(
-            functools.partial(kernel, n, m, p, H, X, C, scale),
+            functools.partial(kernel, n, m, p, H, X, C),
             out_shape=(jax.ShapeDtypeStruct((p, H, X, C), BF16), sums, sums),
             in_specs=[pl.BlockSpec(memory_space=pltpu.HBM)] * 6,
-            out_specs=(vmem, anywhere, anywhere),
+            out_specs=(vmem,) * 3,
             scratch_shapes=scratch
             + [dma((2, nc))] * 4
             + [dma((2, 2, nc))] * 2
             + [dma((2, nc))] * 2
             + [dma((2, nc))] * 8
             + [dma((K,)), dma((2, K)), dma((K,)), dma((K,))]
-            + [dma((2, K)), dma((5,)), dma((2, K))]
+            + [dma((2, K)), dma((5,))]
             + [dma((2, m))] * 2
             + [dma((2, m, nc))] * 4,
             compiler_params=pltpu.CompilerParams(
@@ -633,12 +637,16 @@
             ),
         )(*(pltpu.with_memory_space_constraint(v, pltpu.HBM) for v in (inputs, pre_one, pre_two, cot, filt_one, filt_two)))
         got, one, two = pl.pallas_call(
-            emit,
-            out_shape=tuple(jax.ShapeDtypeStruct(v.shape, v.dtype) for v in made),
+            functools.partial(emit, scale),
+            out_shape=(
+                jax.ShapeDtypeStruct((p, H, X, C), BF16),
+                jax.ShapeDtypeStruct((K, C, C), F32),
+                jax.ShapeDtypeStruct((K, C, C), F32),
+            ),
             in_specs=[vmem] * 3,
             out_specs=(anywhere,) * 3,
-            scratch_shapes=[dma((3,))],
-            compiler_params=pltpu.CompilerParams(vmem_limit_bytes=4 * 1024 * 1024),
+            scratch_shapes=[pltpu.VMEM((2, K, C, C), F32), dma((7,))],
+            compiler_params=pltpu.CompilerParams(vmem_limit_bytes=8 * 1024 * 1024),
         )(*made)
         return got, one.reshape(p, 3, 3, C, C), two.reshape(p, 3, 3, C, C)
 

time: 63.5 us -> 59.5 us (0.937)
  Pallas kernels: 62.5 us -> 58.6 us
    pallas_call x2, Pallas kernels: 62.5 us -> 58.6 us  [the longest x1 57.2 us: shards(): pl.pallas_call(functools.partial(kernel, n, m, p, H, X, C), out_shape=(ja...]
where the time goes in v3:
time: 59.5 us; the launch traced here: 59.3 us
  Pallas kernels  58.6 us (98%)
  between operations  0.64 us (1%)
    pallas_call x1, Pallas kernels, shards(): pl.pallas_call(functools.partial(kernel, n, m, p, H, X, C), out_shape=(ja...  57.2 us
    pallas_call x1, Pallas kernels, shards(): pl.pallas_call(functools.partial(emit, scale), out_shape=(jax.ShapeDtypeS...  1.49 us

profile of v3, /device:TPU:0, one launch (start us, length us, event | category | flops | bytes accessed | tf_op | source)
XLA Modules:
  0.0 59.3 jit_solution(6987617733363802387)
XLA Ops:
  0.6 57.2 %shard_map.85 = (bf16[2,4,32,128]{3,2,1,0:T(8,128)(2,1)S(1)}, bf16[18,128,128]{2,1,0:T(8,128)(2,1)S(1)}, bf16[18,128,128]{2,1,0:T(8,128)(2,1)S(1)}) custom-call(bf16[2,4,32,128]{3,2,1,0:T(8,128)(2,1)} %inputs_at.1, bf16[2,4,32,128]{3,2,1,0:T(8,128)(2,1)} %pre_one_at.1, bf16[2,4,32,128]{3,2,1,0:T(8,128)(2,1)} %pre_two_at.1, bf16[2,4,32,128]{3,2,1,0:T(8,128)(2,1)} %cot_at.1, ...), custom_call_target="tpu_custom_call" | custom-call | tf_op jit(solution)/shard_map/pallas_call | solution.py:621
  57.8 1.5 %shard_map.86 = (bf16[2,4,32,128]{3,2,1,0:T(8,128)(2,1)}, f32[18,128,128]{2,1,0:T(8,128)}, f32[18,128,128]{2,1,0:T(8,128)}) custom-call(bf16[2,4,32,128]{3,2,1,0:T(8,128)(2,1)S(1)} %get-tuple-element.9.got, bf16[18,128,128]{2,1,0:T(8,128)(2,1)S(1)} %get-tuple-element.10.one, bf16[18,128,128]{2,1,0:T(8,128)(2,1)S(1)} %get-tuple-element.11.two), custom_call_target="tpu_custom_call" | custom-call | tf_op jit(solution)/shard_map/pallas_call | solution.py:639

commit v4 on v3

--- a/solution.py
+++ b/solution.py
@@ -349,9 +349,8 @@
             if q in beside:
                 beside[q]()
 
-    def merge_terms(ph):
-        sent = []
-        for t in list(range(1, nc)) + [0]:
+    def merge_terms(ph, ts):
+        for t in ts:
             pltpu.make_async_remote_copy(
                 src_ref=part_x.at[ph, t], dst_ref=part_x.at[ph, t],
                 send_sem=x_ss.at[ph, t], recv_sem=x_rs.at[ph, t],
@@ -364,12 +363,13 @@
                 else:
                     part_m[ph, t, o] = total.astype(BF16)
             if t > 0:
-                sent.append(
+                merged[ph].append(
                     start(
                         copy(part_m.at[ph, t], part_r.at[ph, t], p_ss.at[ph, t], p_rs.at[ph, t], to(t), z)
                     )
                 )
-        return sent
+
+    merged = ([], [])
 
     def part_sum(ph, copies):
         arrive(copies)
@@ -472,7 +472,7 @@
     g_sent = send_grad(0)
     send_cols(0)
     a_sent = send_feat()
-    moves = {(0, m - 1): spread_at(0, m - 1, z, inputs)}
+    moves = {}
 
     def spread(f, *ks):
         for k in ks:
@@ -491,21 +491,23 @@
     data_terms(0, {
         n // 8: lambda: spread(0, 1),
         n // 2: lambda: kept.update(a=relay_feat(a_sent)),
+        n - 2: lambda: merge_terms(0, range(1, max(1, nc // 2))),
     })
     arrive(kept["a"])
     build_lhs()
-    p_sent = merge_terms(0)
+    merge_terms(0, [*range(max(1, nc // 2), nc), 0])
     spread(0, *range(2, m - 1))
+    moves[0, m - 1] = spread_at(0, m - 1, z, inputs)
     filt_terms()
-    relay(0, m - 1, *range(min(2, m - 1)))
-
-    delta = part_sum(0, p_sent).reshape(p, H, X, C)
+    relay(0, *range(min(2, m - 1)))
+
+    delta = part_sum(0, merged[0]).reshape(p, H, X, C)
     grad_one = (delta * turn[...]).astype(BF16).astype(F32)
     stage_grad(1, grad_one)
     g_sent = send_grad(1)
     send_cols(1)
     begin(min(7, 18 // p), 18)
-    relay(0, *range(2, m - 1))
+    relay(0, *range(2, m))
     go_in(0, 7)
     for k in range(m):
         arrive(moves[0, k][1])
@@ -523,16 +525,16 @@
     build_gx(1)
     data_terms(1, {
         n // 4: lambda: spread(1, 1),
-        3 * n // 4: lambda: spread(1, *range(2, m - 1)),
+        3 * n // 4 - 1: lambda: spread(1, *range(2, m - 1)),
+        n - 2: lambda: merge_terms(1, range(1, max(1, nc // 2))),
     })
-    go_in(7, 11)
-    p_sent = merge_terms(1)
+    merge_terms(1, [*range(max(1, nc // 2), nc), 0])
     cols = [moves[1, k][1] for k in range(m - 1)]
     if m == 4:
         turn_col(column(3))
         col_terms(0)
     relay(1, 0)
-    go_in(11, 18)
+    go_in(7, 18)
     cross(0, 7)
     relay(1, *range(1, m - 1))
     if m == 4:
@@ -540,7 +542,7 @@
         col_terms(1)
     settle(0, 7)
     cross(7, 11)
-    out_in[...] = part_sum(1, p_sent).astype(BF16).reshape(p, H, X, C)
+    out_in[...] = part_sum(1, merged[1]).astype(BF16).reshape(p, H, X, C)
     if m == 4:
         arrive(cols[1])
         col_terms(2)

time: 59.5 us -> 59.1 us (level)
  no operation moved by 1% of the time
where the time goes in v4:
time: 59.1 us; the launch traced here: 59 us
  Pallas kernels  58.3 us (99%)
  between operations  0.64 us (1%)
    pallas_call x1, Pallas kernels, shards(): pl.pallas_call(functools.partial(kernel, n, m, p, H, X, C), out_shape=(ja...  56.8 us
    pallas_call x1, Pallas kernels, shards(): pl.pallas_call(functools.partial(emit, scale), out_shape=(jax.ShapeDtypeS...  1.49 us

profile of v4, /device:TPU:0, one launch (start us, length us, event | category | flops | bytes accessed | tf_op | source)
XLA Modules:
  0.0 59.0 jit_solution(10732515408174406712)
XLA Ops:
  0.6 56.8 %shard_map.85 = (bf16[2,4,32,128]{3,2,1,0:T(8,128)(2,1)S(1)}, bf16[18,128,128]{2,1,0:T(8,128)(2,1)S(1)}, bf16[18,128,128]{2,1,0:T(8,128)(2,1)S(1)}) custom-call(bf16[2,4,32,128]{3,2,1,0:T(8,128)(2,1)} %inputs_at.1, bf16[2,4,32,128]{3,2,1,0:T(8,128)(2,1)} %pre_one_at.1, bf16[2,4,32,128]{3,2,1,0:T(8,128)(2,1)} %pre_two_at.1, bf16[2,4,32,128]{3,2,1,0:T(8,128)(2,1)} %cot_at.1, ...), custom_call_target="tpu_custom_call" | custom-call | tf_op jit(solution)/shard_map/pallas_call | solution.py:623
  57.5 1.5 %shard_map.86 = (bf16[2,4,32,128]{3,2,1,0:T(8,128)(2,1)}, f32[18,128,128]{2,1,0:T(8,128)}, f32[18,128,128]{2,1,0:T(8,128)}) custom-call(bf16[2,4,32,128]{3,2,1,0:T(8,128)(2,1)S(1)} %get-tuple-element.9.got, bf16[18,128,128]{2,1,0:T(8,128)(2,1)S(1)} %get-tuple-element.10.one, bf16[18,128,128]{2,1,0:T(8,128)(2,1)S(1)} %get-tuple-element.11.two), custom_call_target="tpu_custom_call" | custom-call | tf_op jit(solution)/shard_map/pallas_call | solution.py:641

commit v5 on v4

--- a/solution.py
+++ b/solution.py
@@ -89,9 +89,6 @@
              (inputs_at, field_in.at[a_at(me, me), z]))
         )
     ]
-    for load in fetch + loads[0] + loads[1]:
-        load.start()
-
     barrier = pltpu.get_barrier_semaphore()
     near_cols = sorted({1 % m, (m - 1) % m})
     partners = [(sib, z)] + [(to(t), z) for t in range(1, nc)]
@@ -102,6 +99,8 @@
             barrier, inc=1, device_id={"rot": rot, "az": az},
             device_id_type=pl.DeviceIdType.MESH,
         )
+    for load in fetch + loads[0] + loads[1]:
+        load.start()
 
     pending = []
     def start(c):

time: 59.1 us -> 59.1 us (level)
  no operation moved by 1% of the time
where the time goes in v5:
time: 59.1 us; the launch traced here: 58.9 us
  Pallas kernels  58.2 us (98%)
  between operations  0.64 us (1%)
    pallas_call x1, Pallas kernels, shards(): pl.pallas_call(functools.partial(kernel, n, m, p, H, X, C), out_shape=(ja...  56.7 us
    pallas_call x1, Pallas kernels, shards(): pl.pallas_call(functools.partial(emit, scale), out_shape=(jax.ShapeDtypeS...  1.49 us

profile of v5, /device:TPU:0, one launch (start us, length us, event | category | flops | bytes accessed | tf_op | source)
XLA Modules:
  0.0 58.9 jit_solution(14640813125377797822)
XLA Ops:
  0.6 56.7 %shard_map.85 = (bf16[2,4,32,128]{3,2,1,0:T(8,128)(2,1)S(1)}, bf16[18,128,128]{2,1,0:T(8,128)(2,1)S(1)}, bf16[18,128,128]{2,1,0:T(8,128)(2,1)S(1)}) custom-call(bf16[2,4,32,128]{3,2,1,0:T(8,128)(2,1)} %inputs_at.1, bf16[2,4,32,128]{3,2,1,0:T(8,128)(2,1)} %pre_one_at.1, bf16[2,4,32,128]{3,2,1,0:T(8,128)(2,1)} %pre_two_at.1, bf16[2,4,32,128]{3,2,1,0:T(8,128)(2,1)} %cot_at.1, ...), custom_call_target="tpu_custom_call" | custom-call | tf_op jit(solution)/shard_map/pallas_call | solution.py:622
  57.4 1.5 %shard_map.86 = (bf16[2,4,32,128]{3,2,1,0:T(8,128)(2,1)}, f32[18,128,128]{2,1,0:T(8,128)}, f32[18,128,128]{2,1,0:T(8,128)}) custom-call(bf16[2,4,32,128]{3,2,1,0:T(8,128)(2,1)S(1)} %get-tuple-element.9.got, bf16[18,128,128]{2,1,0:T(8,128)(2,1)S(1)} %get-tuple-element.10.one, bf16[18,128,128]{2,1,0:T(8,128)(2,1)S(1)} %get-tuple-element.11.two), custom_call_target="tpu_custom_call" | custom-call | tf_op jit(solution)/shard_map/pallas_call | solution.py:640
